TPU v7x, 512 devices: a whole 4x4x16 slice. The times are simulated.
512 devices in a mesh: seq: 32 (over y, x, core), tp: 16 (over z).
Axes of the slice: x: 4, y: 4, z: 16, core: 2. Of those that a mesh axis runs over, the one named last changes fastest.
Arguments:
- tokens: bfloat16 [4096, 4096], P('seq', 'tp'), may hold values from -6 to 6
- in_weight: bfloat16 [4096, 8192], P(None, 'tp'), may hold values from -0.09375 to 0.09375
- conv_weight: float32 [4, 8192], P(None, 'tp'), may hold values from -3 to 3
- conv_bias: float32 [8192], P('tp'), may hold values from -0.5 to 0.5
- proj_weight: bfloat16 [8192, 288], P('tp'), may hold values from -0.0625 to 0.0625
- dt_weight: bfloat16 [256, 8192], P(None, 'tp'), may hold values from -0.375 to 0.375
- dt_bias: float32 [8192], P('tp'), may hold values from -7 to -2
- a_log: float32 [16, 8192], P(None, 'tp'), may hold values from -3 to 1.5
- skip_gain: float32 [8192], P('tp'), may hold values from 0.5 to 1.5
- threshold: float32 [8192], P('tp'), may hold values from -0.5 to 0.5
Outputs:
- gated: bfloat16 [4096, 8192], P('seq', 'tp')
All inputs are finite; a program needn't handle non-finite values.
Results may differ from a plain program's by a relative error of at most 0.0085.
Values may be sent and summed in bfloat16 or wider, within the bound.
No kernel may reach another device: no remote copies, remote signals or barrier semaphores. Data moves between devices by JAX's collectives and lax.ppermute only.
A program may use at most 64 MiB of HBM per device.

v0:
```python
import math
import jax
import jax.numpy as jnp
from jax import lax
from jax.sharding import PartitionSpec as P


def shifted(x, axis, by):
    peers = lax.axis_size(axis)
    pairs = [(i, i + by) for i in range(peers) if 0 <= i + by < peers]
    return lax.ppermute(x, axis, pairs)


def carried_in(value, axis, join, neutral):
    count, mine = (lax.axis_size(axis), lax.axis_index(axis))
    pieces = jax.tree.map(lambda part: lax.all_gather(part, axis), value)
    total = jax.tree.map(
        lambda part, zero: jnp.full_like(part, 0) + jnp.asarray(zero, part.dtype), value, neutral
    )

    def turn(position, total):
        longer = join(total, jax.tree.map(lambda part: part[position], pieces))
        return jax.tree.map(lambda new, old: jnp.where(position < mine, new, old), longer, total)

    return lax.fori_loop(0, count - 1, turn, total)


def combine_pair(earlier, later):
    return (earlier[0] * later[0], later[0] * earlier[1] + later[1])


def lower_table(rows):
    row_ids = lax.broadcasted_iota(jnp.int32, (rows, rows), 0)
    col_ids = lax.broadcasted_iota(jnp.int32, (rows, rows), 1)
    return row_ids >= col_ids


def local_pass(step_size, inflow_rows, b_coef, c_coef, rate, start_state, block):
    rows, width = step_size.shape
    count = rows // block
    lower = lower_table(block)
    lower_float = lower.astype(jnp.float32)

    def run(carry, items):
        state, decay_all = carry
        step_block, flow_block, b_block, c_block = items
        summed = jnp.dot(
            lower_float,
            step_block,
            precision=lax.Precision.HIGHEST,
            preferred_element_type=jnp.float32,
        )
        diff = jnp.where(lower[:, :, None], summed[:, None, :] - summed[None, :, :], 0.0)
        weights = jnp.where(
            lower[:, :, None, None], jnp.exp(diff[:, :, None, :] * rate[None, None]), 0.0
        )
        inflow = flow_block[:, None, :] * b_block[:, :, None]
        states = jnp.einsum("tsnc,snc->tnc", weights, inflow, precision=lax.Precision.HIGHEST)
        states = states + jnp.exp(summed[:, None, :] * rate[None]) * state[None]
        outputs = jnp.einsum("tn,tnc->tc", c_block, states, precision=lax.Precision.HIGHEST)
        block_decay = jnp.exp(summed[-1][None, :] * rate)
        return ((states[-1], block_decay * decay_all), outputs)

    items = (
        step_size.reshape(count, block, width),
        inflow_rows.reshape(count, block, width),
        b_coef.reshape(count, block, -1),
        c_coef.reshape(count, block, -1),
    )
    (end_state, decay_all), outputs = lax.scan(
        run, (start_state, jnp.ones_like(start_state)), items
    )
    return (end_state, decay_all, outputs.reshape(rows, width))


def per_device(
    tokens,
    in_weight,
    conv_weight,
    conv_bias,
    proj_weight,
    dt_weight,
    dt_bias,
    a_log,
    skip_gain,
    threshold,
):
    tok_rows = tokens.shape[0]
    width = in_weight.shape[1]
    taps = conv_weight.shape[0]
    rank = dt_weight.shape[0]
    states_n = a_log.shape[0]
    projected = jnp.dot(
        lax.all_gather(tokens, "tp", axis=1, tiled=True),
        in_weight,
        preferred_element_type=jnp.float32,
    ).astype(jnp.bfloat16)
    rim_inner = shifted(projected[tok_rows - taps + 1 :], "seq", 1)
    padded = jnp.concatenate([rim_inner, projected], axis=0)
    pre = conv_bias[None, :] + jnp.zeros((tok_rows, width), jnp.float32)
    for k in range(taps):
        pre = pre + conv_weight[k][None, :] * padded[k : k + tok_rows].astype(jnp.float32)
    u_half = jax.nn.silu(pre).astype(jnp.bfloat16)
    partial_sums = jnp.dot(u_half, proj_weight, preferred_element_type=jnp.float32)
    total = lax.psum(partial_sums, "tp")
    dt_low = total[:, :rank].astype(jnp.bfloat16)
    b_coef = total[:, rank : rank + states_n]
    c_coef = total[:, rank + states_n :]
    step_size = jax.nn.softplus(
        jnp.dot(dt_low, dt_weight, preferred_element_type=jnp.float32) + dt_bias[None, :]
    )
    rate = -jnp.exp(a_log)
    u_float = u_half.astype(jnp.float32)
    inflow_rows = step_size * u_float
    block = math.gcd(tok_rows, 16)
    zero_state = jnp.zeros((states_n, width), jnp.float32)
    end_state, decay_all, local_out = local_pass(
        step_size, inflow_rows, b_coef, c_coef, rate, zero_state, block
    )
    incoming = carried_in(
        (decay_all, end_state), "seq", combine_pair, (jnp.ones_like(decay_all), zero_state)
    )
    entry_state = incoming[1]
    whole_lower = lower_table(tok_rows).astype(jnp.float32)
    summed = jnp.dot(
        whole_lower, step_size, precision=lax.Precision.HIGHEST, preferred_element_type=jnp.float32
    )
    growth = jnp.exp(summed[:, None, :] * rate[None])
    scan_out = local_out + jnp.einsum(
        "tn,tnc->tc", c_coef, growth * entry_state[None], precision=lax.Precision.HIGHEST
    )
    y_full = scan_out + skip_gain[None, :] * u_float
    return (y_full * jax.nn.sigmoid(4.0 * (y_full - threshold[None, :]))).astype(jnp.bfloat16)


def solution(mesh):
    return jax.shard_map(
        per_device,
        mesh=mesh,
        in_specs=(
            P("seq", "tp"),
            P(None, "tp"),
            P(None, "tp"),
            P("tp"),
            P("tp", None),
            P(None, "tp"),
            P("tp"),
            P(None, "tp"),
            P("tp"),
            P("tp"),
        ),
        out_specs=P("seq", "tp"),
        check_vma=False,
    )
```

profile of v0, /device:TPU:1, one launch (start us, length us, event | category | flops | bytes accessed | tf_op | source)
XLA Modules:
  0.0 405.8 jit_solution(9924214870880622098)
XLA Ops:
  7.3 68.5 %all-gather.6.cloned.1.call-done = bf16[128,4096]{1,0:T(8,128)(2,1)} async-done(((bf16[128,256]{1,0:T(8,128)(2,1)}), bf16[128,4096]{1,0:T(8,128)(2,1)}) %all-gather.6.cloned.1.call-update) | async-done | bytes 1048592 | tf_op jit(solution)/shard_map/all_gather | solution.py:94
  75.8 3.2 convolution_convert_fusion
  79.1 14.8 %collective-permute-start = (bf16[3,512]{1,0:T(4,128)(2,1)S(1)}, bf16[3,512]{1,0:T(4,128)(2,1)S(1)}, u32[]{:S(2)}, u32[]{:S(2)}) collective-permute-start(bf16[3,512]{1,0:T(4,128)(2,1)S(1)} %slice.57), channel_id=1, source_target_pairs={{0,16},{16,32},{32,48},{48,64},{64,80},{80,96},{96,112},{112,128},... | collective-permute-start | bytes 9224 | tf_op jit(solution)/shard_map/ppermute | solution.py:11
  94.9 0.9 fusion.23
  95.9 121.1 %all-reduce.2.cloned.1.call-done = f32[128,288]{0,1:T(8,128)} async-done(((f32[128,288]{0,1:T(8,128)}), f32[128,288]{0,1:T(8,128)}) %all-reduce.2.cloned.1.call-update) | async-done | bytes 147472 | tf_op jit(solution)/shard_map/psum | solution.py:105
  217.9 1.3 convert_multiply_fusion.1
  219.1 25.1 %while.31 = (s32[]{:T(128)}, f32[16,512]{1,0:T(8,128)S(1)}, f32[16,512]{1,0:T(8,128)S(1)}, f32[8,16,512]{2,1,0:T(8,128)S(1)}, f32[8,16,512]{2,1,0:T(8,128)S(1)},...) while((s32[]{:T(128)}, f32[16,512]{1,0:T(8,128)S(1)}, ...), condition=%wide.region_2.3_spmd.clone.clone, body=%wide.region_1.2_spmd.clone.clone.sunk | while | flops 12215043 | bytes 4797323 | solution.py:70
  219.5 2.2 multiply_reduce_fusion.2
  222.7 2.2 multiply_reduce_fusion.2
  225.8 2.2 multiply_reduce_fusion.2
  228.9 2.2 multiply_reduce_fusion.2
  232.1 2.2 multiply_reduce_fusion.2
  235.2 2.2 multiply_reduce_fusion.2
  238.3 2.2 multiply_reduce_fusion.2
  241.5 2.2 multiply_reduce_fusion.2
  245.9 63.7 %all-gather.8.cloned.1.call-done = f32[512,512]{1,0:T(8,128)} async-done(((f32[16,512]{1,0:T(8,128)}), f32[512,512]{1,0:T(8,128)}) %all-gather.8.cloned.1.call-update) | async-done | bytes 1048592 | tf_op jit(solution)/shard_map/all_gather | solution.py:16
  309.6 61.0 %all-gather.10.cloned.1.call-done = f32[512,512]{1,0:T(8,128)} async-done(((f32[16,512]{1,0:T(8,128)}), f32[512,512]{1,0:T(8,128)}) %all-gather.10.cloned.1.call-update) | async-done | bytes 1048592 | tf_op jit(solution)/shard_map/all_gather | solution.py:16
  370.6 25.2 %while.30 = (s32[]{:T(128)}, f32[16,512]{1,0:T(8,128)S(1)}, s32[]{:T(128)}, f32[32,16,512]{2,1,0:T(8,128)}, f32[32,16,512]{2,1,0:T(8,128)}, /*index=5*/s32[]{:T(128)}, s32[]{:T(128)}) while((s32[]{:T(128)}, f32[16,512]{1,0:T(8,128)S(1)}, s32[]{:T(128)}, f32[32,16,512]{2,1,0:T(8,128)}, f32[32,16,512]{2,1,0:T(8,128)}, ...), condition=%wide.region_4.5_spmd.clone, body=%wide.region_3.4_spmd.clone.sunk | while | flops 32772 | bytes 131173 | solution.py:25
  375.5 0.8 fusion.39
  376.3 0.8 fusion.39
  377.1 0.8 fusion.39
  377.9 0.8 fusion.39
  383.6 0.8 fusion.39
  395.8 2.7 fusion.9
  (165 shorter events, 32.3 us)
Async XLA Ops:
  6.5 88.3 %copy-start = (bf16[512,288]{0,1:T(8,128)(2,1)S(1)}, bf16[512,288]{0,1:T(8,128)(2,1)}, u32[]{:S(2)}) copy-start(bf16[512,288]{0,1:T(8,128)(2,1)} %param.18) | copy-start | bytes 884740
  6.5 87.4 %copy-start.5 = (f32[4,512]{1,0:T(4,128)S(1)}, f32[4,512]{1,0:T(4,128)}, u32[]{:S(2)}) copy-start(f32[4,512]{1,0:T(4,128)} %param.16) | copy-start | bytes 24580
  6.5 88.1 %copy-start.6 = (f32[512]{0:T(512)S(1)}, f32[512]{0:T(512)}, u32[]{:S(2)}) copy-start(f32[512]{0:T(512)} %param.17) | copy-start | bytes 6148
  6.5 89.3 %copy-start.4 = (f32[16,512]{1,0:T(8,128)S(1)}, f32[16,512]{1,0:T(8,128)}, u32[]{:S(2)}) copy-start(f32[16,512]{1,0:T(8,128)} %param.21) | copy-start | bytes 98308
  6.5 211.3 %copy-start.3 = (bf16[256,512]{1,0:T(8,128)(2,1)S(1)}, bf16[256,512]{1,0:T(8,128)(2,1)}, u32[]{:S(2)}) copy-start(bf16[256,512]{1,0:T(8,128)(2,1)} %param.19) | copy-start | bytes 786436
  6.5 211.3 %copy-start.7 = (f32[512]{0:T(512)S(1)}, f32[512]{0:T(512)}, u32[]{:S(2)}) copy-start(f32[512]{0:T(512)} %param.20) | copy-start | bytes 6148
  6.6 69.3 %all-gather.6.cloned.1.call-start = ((), (), s32[]{:S(2)}) async-start(), calls=%async_computation | async-start | bytes 1114112 | tf_op jit(solution)/shard_map/all_gather | solution.py:94
  7.3 209.6 %all-reduce.2.cloned.1.call-start = ((), (), s32[]{:S(2)}) async-start(), calls=%async_computation.1 | async-start | bytes 294912 | tf_op jit(solution)/shard_map/psum | solution.py:105
  79.1 15.6 %collective-permute-start = (bf16[3,512]{1,0:T(4,128)(2,1)S(1)}, bf16[3,512]{1,0:T(4,128)(2,1)S(1)}, u32[]{:S(2)}, u32[]{:S(2)}) collective-permute-start(bf16[3,512]{1,0:T(4,128)(2,1)S(1)} %slice.57), channel_id=1, source_target_pairs={{0,16},{16,32},{32,48},{48,64},{64,80},{80,96},{96,112},{112,128},... | collective-permute-start | bytes 9224 | tf_op jit(solution)/shard_map/ppermute | solution.py:11
  95.8 213.8 %all-gather.8.cloned.1.call-start = ((), (), s32[]{:S(2)}) async-start(), calls=%async_computation.2 | async-start | bytes 1081344 | tf_op jit(solution)/shard_map/all_gather | solution.py:16
  244.2 0.6 copy-start.2
  244.2 0.7 copy-start.1
  244.2 154.3 %copy-start.8 = (f32[512]{0:T(512)S(1)}, f32[512]{0:T(512)}, u32[]{:S(2)}) copy-start(f32[512]{0:T(512)} %param.23) | copy-start | bytes 6148
  244.3 154.3 %copy-start.9 = (f32[512]{0:T(512)S(1)}, f32[512]{0:T(512)}, u32[]{:S(2)}) copy-start(f32[512]{0:T(512)} %param.22) | copy-start | bytes 6148
  244.9 125.8 %all-gather.10.cloned.1.call-start = ((), (), s32[]{:S(2)}) async-start(), calls=%async_computation.3 | async-start | bytes 1081344 | tf_op jit(solution)/shard_map/all_gather | solution.py:16
Sparse Core Ops, SparseCore 0:
  9.4 66.3 all-gather.5
  95.9 120.9 all-reduce.1
  245.0 64.5 all-gather.7
  313.1 57.5 all-gather.9
where the time goes:
time: 408 us; the launch traced here: 406 us
  waiting for transfers between devices  316 us (77%)
  other arithmetic  44.8 us (11%)
  starting transfers between devices  15 us (4%)
  between operations  13.4 us (3%)
  matrix products  12.7 us (3%)
    all_gather x2, waiting for transfers between devices, carried_in(): pieces = jax.tree.map(lambda part: lax.all_gather(part, axis), value)  125 us
    psum x1, waiting for transfers between devices, per_device(): total = lax.psum(partial_sums, 'tp')  121 us
    all_gather x1, waiting for transfers between devices, per_device(): lax.all_gather(tokens, 'tp', axis=1, tiled=True)  68.5 us
    select_n x31, other arithmetic, turn(): jnp.where(position < mine, new, old)  24.5 us
    dot_general x8, other arithmetic, run(): jnp.einsum('tsnc,snc->tnc', weights, inflow, precision=lax.Precision.HIGH...  17.3 us
    ppermute x1, starting transfers between devices, shifted(): return lax.ppermute(x, axis, pairs)  14.8 us
  transfers between devices with their start and end apart: 5, of which 5 were waited for; matrix products, arithmetic and copies ran while one was open for 0% of the time, Pallas kernels for 0%

commit v1 on v0

--- a/solution.py
+++ b/solution.py
@@ -102,7 +102,7 @@
         pre = pre + conv_weight[k][None, :] * padded[k : k + tok_rows].astype(jnp.float32)
     u_half = jax.nn.silu(pre).astype(jnp.bfloat16)
     partial_sums = jnp.dot(u_half, proj_weight, preferred_element_type=jnp.float32)
-    total = lax.psum(partial_sums, "tp")
+    total = jnp.sum(lax.all_gather(partial_sums, "tp"), axis=0)
     dt_low = total[:, :rank].astype(jnp.bfloat16)
     b_coef = total[:, rank : rank + states_n]
     c_coef = total[:, rank + states_n :]

time: 408 us -> 355 us (0.87)
  waiting for transfers between devices: 316 us -> 262 us
    psum x1 -> x0, waiting for transfers between devices: 121 us -> none  [per_device(): total = lax.psum(partial_sums, 'tp')]
    all_gather x0 -> x1, waiting for transfers between devices: none -> 67.6 us  [per_device(): total = jnp.sum(lax.all_gather(partial_sums, 'tp'), axis=0)]
where the time goes in v1:
time: 355 us; the launch traced here: 353 us
  waiting for transfers between devices  262 us (74%)
  other arithmetic  45.3 us (13%)
  starting transfers between devices  15 us (4%)
  between operations  13.4 us (4%)
  matrix products  11.8 us (3%)
    all_gather x2, waiting for transfers between devices, carried_in(): pieces = jax.tree.map(lambda part: lax.all_gather(part, axis), value)  124 us
    all_gather x1, waiting for transfers between devices, per_device(): lax.all_gather(tokens, 'tp', axis=1, tiled=True)  68.5 us
    all_gather x1, waiting for transfers between devices, per_device(): total = jnp.sum(lax.all_gather(partial_sums, 'tp'), axis=0)  67.6 us
    select_n x31, other arithmetic, turn(): jnp.where(position < mine, new, old)  24.5 us
    dot_general x8, other arithmetic, run(): jnp.einsum('tsnc,snc->tnc', weights, inflow, precision=lax.Precision.HIGH...  17.3 us
    ppermute x1, starting transfers between devices, shifted(): return lax.ppermute(x, axis, pairs)  14.8 us
  transfers between devices with their start and end apart: 5, of which 5 were waited for; matrix products, arithmetic and copies ran while one was open for 0% of the time, Pallas kernels for 0%

profile of v1, /device:TPU:1, one launch (start us, length us, event | category | flops | bytes accessed | tf_op | source)
XLA Modules:
  0.0 352.5 jit_solution(10806335675563479926)
XLA Ops:
  7.3 68.5 %all-gather.8.cloned.1.call-done = bf16[128,4096]{1,0:T(8,128)(2,1)} async-done(((bf16[128,256]{1,0:T(8,128)(2,1)}), bf16[128,4096]{1,0:T(8,128)(2,1)}) %all-gather.8.cloned.1.call-update) | async-done | bytes 1048592 | tf_op jit(solution)/shard_map/all_gather | solution.py:94
  75.8 3.2 convolution_convert_fusion
  79.1 14.8 %collective-permute-start = (bf16[3,512]{1,0:T(4,128)(2,1)S(1)}, bf16[3,512]{1,0:T(4,128)(2,1)S(1)}, u32[]{:S(2)}, u32[]{:S(2)}) collective-permute-start(bf16[3,512]{1,0:T(4,128)(2,1)S(1)} %slice.57), channel_id=1, source_target_pairs={{0,16},{16,32},{32,48},{48,64},{64,80},{80,96},{96,112},{112,128},... | collective-permute-start | bytes 9224 | tf_op jit(solution)/shard_map/ppermute | solution.py:11
  94.8 0.9 fusion.23
  95.9 67.6 %all-gather.10.cloned.1.call-done = f32[2048,288]{0,1:T(8,128)} async-done(((f32[128,288]{0,1:T(8,128)}), f32[2048,288]{0,1:T(8,128)}) %all-gather.10.cloned.1.call-update) | async-done | bytes 2359312 | tf_op jit(solution)/shard_map/all_gather | solution.py:105
  163.5 2.1 copy.27
  166.6 25.1 %while.31 = (s32[]{:T(128)}, f32[16,512]{1,0:T(8,128)S(1)}, f32[16,512]{1,0:T(8,128)S(1)}, f32[8,16,512]{2,1,0:T(8,128)S(1)}, f32[8,16,512]{2,1,0:T(8,128)S(1)},...) while((s32[]{:T(128)}, f32[16,512]{1,0:T(8,128)S(1)}, ...), condition=%wide.region_2.3_spmd.clone.clone, body=%wide.region_1.2_spmd.clone.clone.sunk | while | flops 12215043 | bytes 4797323 | solution.py:70
  167.0 2.2 multiply_reduce_fusion.2
  170.1 2.2 multiply_reduce_fusion.2
  173.3 2.2 multiply_reduce_fusion.2
  176.4 2.2 multiply_reduce_fusion.2
  179.5 2.2 multiply_reduce_fusion.2
  182.7 2.2 multiply_reduce_fusion.2
  185.8 2.2 multiply_reduce_fusion.2
  188.9 2.2 multiply_reduce_fusion.2
  193.3 63.4 %all-gather.12.cloned.1.call-done = f32[512,512]{1,0:T(8,128)} async-done(((f32[16,512]{1,0:T(8,128)}), f32[512,512]{1,0:T(8,128)}) %all-gather.12.cloned.1.call-update) | async-done | bytes 1048592 | tf_op jit(solution)/shard_map/all_gather | solution.py:16
  256.7 60.5 %all-gather.14.cloned.1.call-done = f32[512,512]{1,0:T(8,128)} async-done(((f32[16,512]{1,0:T(8,128)}), f32[512,512]{1,0:T(8,128)}) %all-gather.14.cloned.1.call-update) | async-done | bytes 1048592 | tf_op jit(solution)/shard_map/all_gather | solution.py:16
  317.2 25.3 %while.30 = (s32[]{:T(128)}, f32[16,512]{1,0:T(8,128)S(1)}, s32[]{:T(128)}, f32[32,16,512]{2,1,0:T(8,128)}, f32[32,16,512]{2,1,0:T(8,128)}, /*index=5*/s32[]{:T(128)}, s32[]{:T(128)}) while((s32[]{:T(128)}, f32[16,512]{1,0:T(8,128)S(1)}, s32[]{:T(128)}, f32[32,16,512]{2,1,0:T(8,128)}, f32[32,16,512]{2,1,0:T(8,128)}, ...), condition=%wide.region_4.5_spmd.clone, body=%wide.region_3.4_spmd.clone.sunk | while | flops 32772 | bytes 131173 | solution.py:25
  318.0 0.8 fusion.39
  318.8 0.8 fusion.39
  319.7 0.8 fusion.39
  320.5 0.8 fusion.39
  321.3 0.8 fusion.39
  342.5 2.7 fusion.9
  (167 shorter events, 32.4 us)
Async XLA Ops:
  6.5 88.3 %copy-start = (bf16[512,288]{0,1:T(8,128)(2,1)S(1)}, bf16[512,288]{0,1:T(8,128)(2,1)}, u32[]{:S(2)}) copy-start(bf16[512,288]{0,1:T(8,128)(2,1)} %param.18) | copy-start | bytes 884740
  6.5 87.4 %copy-start.5 = (f32[4,512]{1,0:T(4,128)S(1)}, f32[4,512]{1,0:T(4,128)}, u32[]{:S(2)}) copy-start(f32[4,512]{1,0:T(4,128)} %param.16) | copy-start | bytes 24580
  6.5 88.1 %copy-start.6 = (f32[512]{0:T(512)S(1)}, f32[512]{0:T(512)}, u32[]{:S(2)}) copy-start(f32[512]{0:T(512)} %param.17) | copy-start | bytes 6148
  6.5 89.3 %copy-start.4 = (f32[16,512]{1,0:T(8,128)S(1)}, f32[16,512]{1,0:T(8,128)}, u32[]{:S(2)}) copy-start(f32[16,512]{1,0:T(8,128)} %param.21) | copy-start | bytes 98308
  6.5 69.3 %all-gather.8.cloned.1.call-start = ((), (), s32[]{:S(2)}) async-start(), calls=%async_computation | async-start | bytes 1114112 | tf_op jit(solution)/shard_map/all_gather | solution.py:94
  7.3 156.2 %all-gather.10.cloned.1.call-start = ((), (), s32[]{:S(2)}) async-start(), calls=%async_computation.1 | async-start | bytes 2506752 | tf_op jit(solution)/shard_map/all_gather | solution.py:105
  79.1 15.6 %collective-permute-start = (bf16[3,512]{1,0:T(4,128)(2,1)S(1)}, bf16[3,512]{1,0:T(4,128)(2,1)S(1)}, u32[]{:S(2)}, u32[]{:S(2)}) collective-permute-start(bf16[3,512]{1,0:T(4,128)(2,1)S(1)} %slice.57), channel_id=1, source_target_pairs={{0,16},{16,32},{32,48},{48,64},{64,80},{80,96},{96,112},{112,128},... | collective-permute-start | bytes 9224 | tf_op jit(solution)/shard_map/ppermute | solution.py:11
  94.6 71.6 %copy-start.3 = (bf16[256,512]{1,0:T(8,128)(2,1)S(1)}, bf16[256,512]{1,0:T(8,128)(2,1)}, u32[]{:S(2)}) copy-start(bf16[256,512]{1,0:T(8,128)(2,1)} %param.19) | copy-start | bytes 786436
  94.6 71.6 %copy-start.7 = (f32[512]{0:T(512)S(1)}, f32[512]{0:T(512)}, u32[]{:S(2)}) copy-start(f32[512]{0:T(512)} %param.20) | copy-start | bytes 6148
  95.8 160.9 %all-gather.12.cloned.1.call-start = ((), (), s32[]{:S(2)}) async-start(), calls=%async_computation.2 | async-start | bytes 1081344 | tf_op jit(solution)/shard_map/all_gather | solution.py:16
  191.7 0.6 copy-start.2
  191.7 0.7 copy-start.1
  191.7 153.5 %copy-start.8 = (f32[512]{0:T(512)S(1)}, f32[512]{0:T(512)}, u32[]{:S(2)}) copy-start(f32[512]{0:T(512)} %param.23) | copy-start | bytes 6148
  191.7 153.5 %copy-start.9 = (f32[512]{0:T(512)S(1)}, f32[512]{0:T(512)}, u32[]{:S(2)}) copy-start(f32[512]{0:T(512)} %param.22) | copy-start | bytes 6148
  192.3 124.9 %all-gather.14.cloned.1.call-start = ((), (), s32[]{:S(2)}) async-start(), calls=%async_computation.3 | async-start | bytes 1081344 | tf_op jit(solution)/shard_map/all_gather | solution.py:16
Sparse Core Ops, SparseCore 0:
  9.4 66.3 all-gather.7
  95.9 67.5 all-gather.9
  192.4 64.1 all-gather.11
  259.7 57.5 all-gather.13
